TPU v7x, 32 devices: a whole 2x2x4 slice. The times are simulated.
32 devices in a mesh: ctx: 8 (over z, y), head: 4 (over x, core).
Axes of the slice: x: 2, y: 2, z: 4, core: 2. Of those that a mesh axis runs over, the one named last changes fastest.
Arguments:
- tokens: bfloat16 [4096, 2048], P('ctx', 'head'), may hold values from -6 to 6
- value_weight: bfloat16 [2048, 4096], P('ctx', 'head'), may hold values from -0.125 to 0.125
- queries: bfloat16 [4096, 128], P('ctx'), may hold values from -2.390625 to 2.390625
- key_vectors: bfloat16 [4096, 128], P('ctx'), may hold values from -2.390625 to 2.390625
- level_weight: float32 [13, 64, 4096], P(None, 'head', 'ctx'), may hold values from 0.2 to 1
Outputs:
- attended: bfloat16 [4096, 4096], P('ctx', 'head')
All inputs are finite; a program needn't handle non-finite values.
Results may differ from a plain program's by a relative error of at most 0.006.
Values may be sent and summed in bfloat16 or wider, within the bound.
No kernel may reach another device: no remote copies, remote signals or barrier semaphores. Data moves between devices by JAX's collectives and lax.ppermute only.
A program may use at most 64 MiB of HBM per device.

v0:
```python
import jax
import jax.numpy as jnp
from jax import lax
from jax.sharding import PartitionSpec as P


def from_partner(block, axis, distance):
    count = lax.axis_size(axis)
    route = []
    for low in range(count):
        high = low | 1 << distance
        if high != low and high < count:
            route += [(low, high), (high, low)]
    return lax.ppermute(block, axis, route)


def body(tokens, value_weight, queries, key_vectors, level_weight):
    features = lax.all_gather(tokens, "head", axis=1, tiled=True)
    length = features.shape[0]
    width_local = value_weight.shape[1]
    head_local = level_weight.shape[1]
    head_size = width_local // head_local
    state_rows = queries.shape[1]
    stretch_bits = length.bit_length() - 1
    ctx_count = lax.axis_size("ctx")
    dev_bits = ctx_count.bit_length() - 1
    values = jnp.dot(
        features,
        lax.all_gather(value_weight, "ctx", axis=0, tiled=True),
        preferred_element_type=jnp.float32,
    ).astype(jnp.bfloat16)
    tile_len = min(128, length)
    tile_count = length // tile_len
    tile_bits = tile_len.bit_length() - 1
    q_tiles = queries.reshape(tile_count, tile_len, state_rows)
    k_tiles = key_vectors.reshape(tile_count, tile_len, state_rows)
    v_tiles = values.reshape(tile_count, tile_len, width_local)
    tile_scores = jnp.einsum(
        "bin,bjn->bij", q_tiles, k_tiles, preferred_element_type=jnp.float32
    ).astype(jnp.bfloat16)
    row_pos = lax.broadcasted_iota(jnp.int32, (tile_len, tile_len), 0)
    col_pos = lax.broadcasted_iota(jnp.int32, (tile_len, tile_len), 1)
    differ = jnp.bitwise_xor(row_pos, col_pos)
    pair_level = jnp.zeros((tile_len, tile_len), jnp.int32)
    for bit_num in range(tile_bits):
        pair_level = pair_level + (jnp.right_shift(differ, bit_num) > 0).astype(jnp.int32)
    causal = col_pos <= row_pos
    result = jnp.zeros((length, head_local, head_size), jnp.float32)
    for level_num in range(0, tile_bits + 1):
        scale = 1.0 if level_num == 0 else 2.0 ** (-(level_num - 1) / 2.0)
        chosen = causal & (pair_level == level_num)
        masked = jnp.where(chosen[None], tile_scores, jnp.zeros_like(tile_scores))
        mixed = jnp.einsum("bij,bjc->bic", masked, v_tiles, preferred_element_type=jnp.float32)
        weights = level_weight[level_num].T * scale
        result = result + weights[..., None] * mixed.reshape(length, head_local, head_size)
    for level_num in range(tile_bits + 1, stretch_bits + 1):
        half_len = 2 ** (level_num - 1)
        groups = length // (2 * half_len)
        scale = 2.0 ** (-(level_num - 1) / 2.0)
        q_right = queries.reshape(groups, 2, half_len, state_rows)[:, 1]
        k_left = key_vectors.reshape(groups, 2, half_len, state_rows)[:, 0]
        v_left = values.reshape(groups, 2, half_len, width_local)[:, 0]
        scores = jnp.einsum(
            "bin,bjn->bij", q_right, k_left, preferred_element_type=jnp.float32
        ).astype(jnp.bfloat16)
        mixed = jnp.einsum("bij,bjc->bic", scores, v_left, preferred_element_type=jnp.float32)
        weights = level_weight[level_num].T.reshape(groups, 2, half_len, head_local)[:, 1] * scale
        addend = weights[..., None] * mixed.reshape(groups, half_len, head_local, head_size)
        result = result.reshape(groups, 2, half_len, head_local, head_size).at[:, 1].add(addend)
        result = result.reshape(length, head_local, head_size)
    state = jnp.einsum("tn,tc->nc", key_vectors, values, preferred_element_type=jnp.float32)
    my_index = lax.axis_index("ctx")
    running = state
    level_states = []
    for section_bit in range(dev_bits):
        partner = from_partner(running, "ctx", section_bit)
        is_right = my_index // 2**section_bit % 2 == 1
        level_states.append(jnp.where(is_right, partner, jnp.zeros_like(partner)))
        running = running + partner
    for section_bit in range(dev_bits):
        level_num = stretch_bits + 1 + section_bit
        scale = 2.0 ** (-(level_num - 1) / 2.0)
        state_high = level_states[section_bit].astype(jnp.bfloat16)
        state_low = (level_states[section_bit] - state_high.astype(jnp.float32)).astype(
            jnp.bfloat16
        )
        reading = jnp.dot(queries, state_high, preferred_element_type=jnp.float32)
        reading = reading + jnp.dot(queries, state_low, preferred_element_type=jnp.float32)
        weights = level_weight[level_num].T * scale
        result = result + weights[..., None] * reading.reshape(length, head_local, head_size)
    return result.reshape(length, width_local).astype(jnp.bfloat16)


def solution(mesh):
    return jax.shard_map(
        body,
        mesh=mesh,
        in_specs=(
            P("ctx", "head"),
            P("ctx", "head"),
            P("ctx", None),
            P("ctx", None),
            P(None, "head", "ctx"),
        ),
        out_specs=P("ctx", "head"),
        check_vma=False,
    )
```

profile of v0, /device:TPU:0, one launch (start us, length us, event | category | flops | bytes accessed | tf_op | source)
XLA Modules:
  0.0 205.0 jit_solution(3942225557572144632)
XLA Ops:
  8.1 1.6 multiply_bitcast_fusion.2
  21.2 13.0 %all-gather.3.cloned.1.call-done = bf16[512,2048]{1,0:T(8,128)(2,1)} async-done(((bf16[512,512]{1,0:T(8,128)(2,1)}), bf16[512,2048]{1,0:T(8,128)(2,1)}) %all-gather.3.cloned.1.call-update) | async-done | bytes 2097168 | tf_op jit(solution)/shard_map/all_gather | solution.py:18
  34.2 75.0 %all-gather.5.cloned.1.call-done = bf16[2048,1024]{1,0:T(8,128)(2,1)} async-done(((bf16[256,1024]{1,0:T(8,128)(2,1)}), bf16[2048,1024]{1,0:T(8,128)(2,1)}) %all-gather.5.cloned.1.call-update) | async-done | bytes 4194320 | tf_op jit(solution)/shard_map/all_gather | solution.py:29
  109.2 5.1 %convolution_convert_fusion = bf16[512,1024]{1,0:T(8,128)(2,1)S(1)} fusion(bf16[512,2048]{1,0:T(8,128)(2,1)} %all-gather.3.cloned.1.call-done, bf16[2048,1024]{1,0:T(8,128)(2,1)} %all-gather.5.cloned.1.call-done), kind=kOutput, calls=%fused_computation.8 | convolution fusion | flops 2148007936 | bytes 7340032 | tf_op jit(solution)/shard_map/dot_general | solution.py:27
  114.3 1.3 convolution_bitcast_fusion
  115.6 1.2 fusion.37
  116.9 1.9 fusion.35
  118.8 1.8 fusion.33
  120.6 1.9 fusion.31
  122.5 1.9 fusion.29
  124.4 1.9 fusion.27
  126.3 1.9 fusion.41
  128.2 1.9 fusion.39
  130.1 1.4 fusion.8
  131.5 7.9 %multiply_add_fusion = f32[2,2,128,16,64]{2,4,3,1,0:T(8,128)S(1)} fusion(f32[2,2,128,16,64]{2,4,3,1,0:T(8,128)} %bitcast.204, f32[2,2,128,16,64]{2,4,3,1,0:T(8,128)} %bitcast.203, f32[2,2,128,16,64]{2,4,3,1,0:T(8,128)} %bitcast.202, f32[2,2,128,16,64]{2,4,3,1,0:T(8,128)} %bitcast.201, f32[2,2,128,16,64]{2,4,3,1,0:T(8,128)} %bitcast.200, ...), kind=kLoop, calls=%fused_computation.7 | loop fusion | flops 7864320 | bytes 19136512 | tf_op jit(solution)/shard_map/add | solution.py:55
  139.8 3.2 %copy.41 = f32[2,2,128,16,64]{2,1,4,3,0:T(2,128)} copy(f32[2,2,128,16,64]{2,4,3,1,0:T(8,128)S(1)} %fusion.9) | data formatting | bytes 4194304 | tf_op jit(solution)/shard_map/scatter-add | solution.py:69
  142.9 2.9 %reshape_reshape.3 = f32[1,2,256,16,64]{2,4,3,1,0:T(8,128)S(1)} reshape(f32[2,2,128,16,64]{2,1,4,3,0:T(2,128)} %copy.41) | data formatting | bytes 4194304 | tf_op jit(solution)/shard_map/reshape;reshape | solution.py:69
  147.3 1.2 copy.43
  149.1 1.6 copy.44
  150.9 7.8 %collective-permute-done = f32[128,1024]{0,1:T(8,128)} collective-permute-done((f32[128,1024]{0,1:T(8,128)}, f32[128,1024]{0,1:T(8,128)}, u32[]{:S(2)}, u32[]{:S(2)}) %collective-permute-start) | collective-permute-done | bytes 524320 | tf_op jit(solution)/shard_map/ppermute | solution.py:14
  161.4 10.0 %collective-permute-done.1 = f32[128,1024]{0,1:T(8,128)S(1)} collective-permute-done((f32[128,1024]{0,1:T(8,128)S(1)}, f32[128,1024]{0,1:T(8,128)S(1)}, u32[]{:S(2)}, u32[]{:S(2)}) %collective-permute-start.1) | collective-permute-done | bytes 524320 | tf_op jit(solution)/shard_map/ppermute | solution.py:14
  171.5 3.0 %collective-permute-start.2 = (f32[128,1024]{0,1:T(8,128)S(1)}, f32[128,1024]{0,1:T(8,128)S(1)}, u32[]{:S(2)}, u32[]{:S(2)}) collective-permute-start(f32[128,1024]{0,1:T(8,128)S(1)} %add.368), channel_id=1, source_target_pairs={{0,16},{16,0},{4,20},{20,4},{8,24},{24,8},{12,28},{28,12},{1,17},{... | collective-permute-start | bytes 1572872 | tf_op jit(solution)/shard_map/ppermute | solution.py:14
  175.4 20.2 %collective-permute-done.2 = f32[128,1024]{0,1:T(8,128)S(1)} collective-permute-done((f32[128,1024]{0,1:T(8,128)S(1)}, f32[128,1024]{0,1:T(8,128)S(1)}, u32[]{:S(2)}, u32[]{:S(2)}) %collective-permute-start.2) | collective-permute-done | bytes 524320 | tf_op jit(solution)/shard_map/ppermute | solution.py:14
  196.9 1.3 copy.45
  (79 shorter events, 20.3 us)
Async XLA Ops:
  6.5 14.5 %copy-start = (bf16[512,128]{1,0:T(8,128)(2,1)S(1)}, bf16[512,128]{1,0:T(8,128)(2,1)}, u32[]{:S(2)}) copy-start(bf16[512,128]{1,0:T(8,128)(2,1)} %param.11) | copy-start | bytes 393220
  6.5 14.5 %copy-start.3 = (bf16[512,128]{1,0:T(8,128)(2,1)S(1)}, bf16[512,128]{1,0:T(8,128)(2,1)}, u32[]{:S(2)}) copy-start(bf16[512,128]{1,0:T(8,128)(2,1)} %param.12) | copy-start | bytes 393220
  6.5 27.7 %all-gather.3.cloned.1.call-start = ((), (), s32[]{:S(2)}) async-start(), calls=%async_computation | async-start | bytes 2621440 | tf_op jit(solution)/shard_map/all_gather | solution.py:18
  7.3 101.9 %all-gather.5.cloned.1.call-start = ((), (), s32[]{:S(2)}) async-start(), calls=%async_computation.1 | async-start | bytes 4718592 | tf_op jit(solution)/shard_map/all_gather | solution.py:29
  114.3 2.5 %copy-start.14 = (pred[128,128]{1,0:T(8,128)(4,1)S(1)}, pred[128,128]{1,0:T(8,128)(4,1)}, u32[]{:S(2)}) copy-start(pred[128,128]{1,0:T(8,128)(4,1)} %fusion.62) | copy-start | bytes 49156
  116.9 1.9 copy-start.13
  118.8 1.9 copy-start.12
  120.6 1.9 copy-start.11
  122.5 1.9 copy-start.10
  124.4 1.9 copy-start.9
  126.3 1.9 copy-start.8
  131.5 7.9 %copy-start.1 = (f32[2,128,1024]{1,2,0:T(8,128)S(1)}, f32[2,128,1024]{1,2,0:T(8,128)}, u32[]{:S(2)}) copy-start(f32[2,128,1024]{1,2,0:T(8,128)} %fusion.8) | copy-start | bytes 3145732
  131.5 7.9 %copy-start.7 = (f32[2,128,16]{1,2,0:T(8,128)S(1)}, f32[2,128,16]{1,2,0:T(8,128)}, u32[]{:S(2)}) copy-start(f32[2,128,16]{1,2,0:T(8,128)} %fusion.82) | copy-start | bytes 49156
  145.9 12.8 %collective-permute-start = (f32[128,1024]{0,1:T(8,128)}, f32[128,1024]{0,1:T(8,128)}, u32[]{:S(2)}, u32[]{:S(2)}) collective-permute-start(f32[128,1024]{0,1:T(8,128)} %convolution_bitcast_fusion), channel_id=1, source_target_pairs={{0,4},{4,0},{8,12},{12,8},{16,20},{20,16},{24,28},{28,24},{1,5},{5... | collective-permute-start | bytes 1572872 | tf_op jit(solution)/shard_map/ppermute | solution.py:14
  150.7 8.0 %copy-start.2 = (f32[128,1024]{0,1:T(8,128)S(1)}, f32[128,1024]{0,1:T(8,128)}, u32[]{:S(2)}) copy-start(f32[128,1024]{0,1:T(8,128)} %convolution_bitcast_fusion) | copy-start | bytes 1572868
  159.8 11.7 %collective-permute-start.1 = (f32[128,1024]{0,1:T(8,128)S(1)}, f32[128,1024]{0,1:T(8,128)S(1)}, u32[]{:S(2)}, u32[]{:S(2)}) collective-permute-start(f32[128,1024]{0,1:T(8,128)S(1)} %add.363), channel_id=1, source_target_pairs={{0,8},{8,0},{4,12},{12,4},{16,24},{24,16},{20,28},{28,20},{1,9},{9... | collective-permute-start | bytes 1572872 | tf_op jit(solution)/shard_map/ppermute | solution.py:14
  171.5 24.0 %collective-permute-start.2 = (f32[128,1024]{0,1:T(8,128)S(1)}, f32[128,1024]{0,1:T(8,128)S(1)}, u32[]{:S(2)}, u32[]{:S(2)}) collective-permute-start(f32[128,1024]{0,1:T(8,128)S(1)} %add.368), channel_id=1, source_target_pairs={{0,16},{16,0},{4,20},{20,4},{8,24},{24,8},{12,28},{28,12},{1,17},{... | collective-permute-start | bytes 1572872 | tf_op jit(solution)/shard_map/ppermute | solution.py:14
  174.9 21.1 %copy-start.4 = (f32[512,16]{0,1:T(8,128)S(1)}, f32[512,16]{0,1:T(8,128)}, u32[]{:S(2)}) copy-start(f32[512,16]{0,1:T(8,128)} %get-tuple-element.29) | copy-start | bytes 98308
  174.9 21.1 %copy-start.5 = (f32[512,16]{0,1:T(8,128)S(1)}, f32[512,16]{0,1:T(8,128)}, u32[]{:S(2)}) copy-start(f32[512,16]{0,1:T(8,128)} %get-tuple-element.40) | copy-start | bytes 98308
  175.0 21.1 %copy-start.6 = (f32[512,16]{0,1:T(8,128)S(1)}, f32[512,16]{0,1:T(8,128)}, u32[]{:S(2)}) copy-start(f32[512,16]{0,1:T(8,128)} %get-tuple-element.41) | copy-start | bytes 98308
Sparse Core Ops, SparseCore 0:
  8.9 25.2 all-gather.2
  36.3 72.7 all-gather.4
where the time goes:
time: 205 us
  waiting for transfers between devices  127 us (62%)
  matrix products  26 us (13%)
  other arithmetic  17.1 us (8%)
  local copies, waits for them, and re-layouts  16.5 us (8%)
  between operations  13.7 us (7%)
  starting transfers between devices  4.38 us (2%)
    all_gather x1, waiting for transfers between devices, body(): lax.all_gather(value_weight, 'ctx', axis=0, tiled=True)  75 us
    ppermute x3, waiting for transfers between devices, from_partner(): return lax.ppermute(block, axis, route)  38 us
    dot_general x8, matrix products, body(): jnp.einsum('bij,bjc->bic', masked, v_tiles, preferred_element_type=jnp.fl...  14.4 us
    all_gather x1, waiting for transfers between devices, body(): features = lax.all_gather(tokens, 'head', axis=1, tiled=True)  13 us
    add x1, other arithmetic, body(): result + weights[..., None] * mixed.reshape(length, head_local, head_size)  7.87 us
    and x8, other arithmetic, body(): chosen = causal & (pair_level == level_num)  5.44 us
    dot_general x1, matrix products, body(): jnp.dot(features, lax.all_gather(value_weight, 'ctx', axis=0, tiled=True)...  5.15 us
    mul x16, local copies, waits for them, and re-layouts, body(): weights[..., None] * mixed.reshape(length, head_local, head_size)  5.08 us
  transfers between devices with their start and end apart: 5, of which 5 were waited for; matrix products, arithmetic and copies ran while one was open for 9% of the time, Pallas kernels for 0%

commit v1 on v0

--- a/solution.py
+++ b/solution.py
@@ -15,7 +15,12 @@
 
 
 def body(tokens, value_weight, queries, key_vectors, level_weight):
-    features = lax.all_gather(tokens, "head", axis=1, tiled=True)
+    ring = [tokens]
+    for hop in range(3):
+        ring.append(lax.ppermute(ring[-1], "head", [(dev, (dev + 1) % 4) for dev in range(4)]))
+    features = jnp.roll(
+        jnp.concatenate(ring[::-1], axis=1), (lax.axis_index("head") + 1) * ring[0].shape[1], axis=1
+    )
     length = features.shape[0]
     width_local = value_weight.shape[1]
     head_local = level_weight.shape[1]

time: 205 us -> 181 us (0.88)
  waiting for transfers between devices: 127 us -> 93 us
  local copies, waits for them, and re-layouts: 16.5 us -> 23.7 us
  starting transfers between devices: 4.38 us -> 7.49 us
    all_gather x1, waiting for transfers between devices: 75 us -> 43 us  [body(): lax.all_gather(value_weight, 'ctx', axis=0, tiled=True)]
    all_gather x1 -> x0, waiting for transfers between devices: 13 us -> none  [body(): features = lax.all_gather(tokens, 'head', axis=1, tiled=True)]
    ppermute x0 -> x3, waiting for transfers between devices: none -> 11.3 us  [body(): lax.ppermute(ring[-1], 'head', [(dev, (dev + 1) % 4) for dev in range(4)])]
    unnamed x31 -> x42, local copies, waits for them, and re-layouts: 0.23 us -> 6.57 us
    ppermute x0 -> x3, starting transfers between devices: none -> 3.14 us  [body(): lax.ppermute(ring[-1], 'head', [(dev, (dev + 1) % 4) for dev in range(4)])]
  transfers between devices with their start and end apart: 5 -> 7, of which waited for: 5 -> 6; matrix products, arithmetic and copies ran while one was open for 9% -> 15% of each run, Pallas kernels for 0% -> 0%
where the time goes in v1:
time: 181 us; the launch traced here: 180 us
  waiting for transfers between devices  93 us (51%)
  matrix products  25.3 us (14%)
  local copies, waits for them, and re-layouts  23.7 us (13%)
  other arithmetic  17 us (9%)
  between operations  13.7 us (8%)
  starting transfers between devices  7.49 us (4%)
    all_gather x1, waiting for transfers between devices, body(): lax.all_gather(value_weight, 'ctx', axis=0, tiled=True)  43 us
    ppermute x3, waiting for transfers between devices, from_partner(): return lax.ppermute(block, axis, route)  38 us
    dot_general x8, matrix products, body(): jnp.einsum('bij,bjc->bic', masked, v_tiles, preferred_element_type=jnp.fl...  13.7 us
    ppermute x3, waiting for transfers between devices, body(): lax.ppermute(ring[-1], 'head', [(dev, (dev + 1) % 4) for dev in range(4)])  11.3 us
    add x1, other arithmetic, body(): result + weights[..., None] * mixed.reshape(length, head_local, head_size)  7.87 us
    unnamed x42, local copies, waits for them, and re-layouts  6.57 us
    and x8, other arithmetic, body(): chosen = causal & (pair_level == level_num)  5.44 us
    dot_general x1, matrix products, body(): jnp.dot(features, lax.all_gather(value_weight, 'ctx', axis=0, tiled=True)...  5.16 us
  transfers between devices with their start and end apart: 7, of which 6 were waited for; matrix products, arithmetic and copies ran while one was open for 15% of the time, Pallas kernels for 0%

profile of v1, /device:TPU:0, one launch (start us, length us, event | category | flops | bytes accessed | tf_op | source)
XLA Modules:
  0.0 180.2 jit_solution(7843981701105963360)
XLA Ops:
  7.8 1.6 multiply_bitcast_fusion.2
  17.4 2.6 %collective-permute-start.1 = (bf16[512,512]{1,0:T(8,128)(2,1)S(1)}, bf16[512,512]{1,0:T(8,128)(2,1)S(1)}, u32[]{:S(2)}, u32[]{:S(2)}) collective-permute-start(bf16[512,512]{1,0:T(8,128)(2,1)S(1)} %collective-permute-done), channel_id=1, source_target_pairs={{0,1},{1,2},{2,3},{3,0},{4,5},{5,6},{6,7},{7,4},{8,9},{9,10},{10,1... | collective-permute-start | bytes 1572872 | tf_op jit(solution)/shard_map/ppermute | solution.py:20
  22.6 3.6 %collective-permute-done.1 = bf16[512,512]{1,0:T(8,128)(2,1)S(1)} collective-permute-done((bf16[512,512]{1,0:T(8,128)(2,1)S(1)}, bf16[512,512]{1,0:T(8,128)(2,1)S(1)}, u32[]{:S(2)}, u32[]{:S(2)}) %collective-permute-start.1) | collective-permute-done | bytes 524320 | tf_op jit(solution)/shard_map/ppermute | solution.py:20
  27.1 7.7 %collective-permute-done.2 = bf16[512,512]{1,0:T(8,128)(2,1)S(1)} collective-permute-done((bf16[512,512]{1,0:T(8,128)(2,1)S(1)}, bf16[512,512]{1,0:T(8,128)(2,1)S(1)}, u32[]{:S(2)}, u32[]{:S(2)}) %collective-permute-start.2) | collective-permute-done | bytes 524320 | tf_op jit(solution)/shard_map/ppermute | solution.py:20
  42.0 43.0 %all-gather.2.cloned.1.call-done = bf16[2048,1024]{1,0:T(8,128)(2,1)} async-done(((bf16[256,1024]{1,0:T(8,128)(2,1)}), bf16[2048,1024]{1,0:T(8,128)(2,1)}) %all-gather.2.cloned.1.call-update) | async-done | bytes 4194320 | tf_op jit(solution)/shard_map/all_gather | solution.py:34
  85.0 5.2 %fusion.6 = bf16[512,1024]{1,0:T(8,128)(2,1)S(1)} fusion(bf16[2048,1024]{1,0:T(8,128)(2,1)} %all-gather.2.cloned.1.call-done, bf16[512,4096]{1,0:T(8,128)(2,1)} %constant_dynamic-update-slice_fusion, s32[]{:T(128)S(6)} %select_n.82), kind=kOutput, calls=%fused_computation.10 | convolution fusion | flops 2148007936 | bytes 7340036 | tf_op jit(solution)/shard_map/dot_general | solution.py:32
  90.2 1.3 convolution_bitcast_fusion
  92.0 1.9 %fusion.34 = f32[4,128,1024]{1,2,0:T(8,128)} fusion(bf16[4,128,1024]{2,1,0:T(8,128)(2,1)S(1)} %bitcast.186, bf16[4,128,128]{2,1,0:T(8,128)(2,1)S(1)} %convolution_convert_fusion.1, pred[128,128]{1,0:T(8,128)(4,1)S(1)} %copy-done.11), kind=kOutput, calls=%fused_computation.50 | convolution fusion | flops 134283264 | bytes 3293184 | tf_op jit(solution)/shard_map/bij,bjc->bic/dot_general | solution.py:58
  93.9 1.8 %fusion.36 = f32[4,128,1024]{1,2,0:T(8,128)} fusion(bf16[4,128,1024]{2,1,0:T(8,128)(2,1)S(1)} %bitcast.187, bf16[4,128,128]{2,1,0:T(8,128)(2,1)S(1)} %convolution_convert_fusion.1, pred[128,128]{1,0:T(8,128)(4,1)S(1)} %copy-done.10), kind=kOutput, calls=%fused_computation.52 | convolution fusion | flops 134283264 | bytes 3293184 | tf_op jit(solution)/shard_map/bij,bjc->bic/dot_general | solution.py:58
  95.7 1.9 %fusion.38 = f32[4,128,1024]{1,2,0:T(8,128)} fusion(bf16[4,128,1024]{2,1,0:T(8,128)(2,1)S(1)} %bitcast.188, bf16[4,128,128]{2,1,0:T(8,128)(2,1)S(1)} %convolution_convert_fusion.1, pred[128,128]{1,0:T(8,128)(4,1)S(1)} %copy-done.9), kind=kOutput, calls=%fused_computation.54 | convolution fusion | flops 134283264 | bytes 3293184 | tf_op jit(solution)/shard_map/bij,bjc->bic/dot_general | solution.py:58
  97.6 1.9 %fusion.40 = f32[4,128,1024]{1,2,0:T(8,128)} fusion(bf16[4,128,1024]{2,1,0:T(8,128)(2,1)S(1)} %bitcast.189, bf16[4,128,128]{2,1,0:T(8,128)(2,1)S(1)} %convolution_convert_fusion.1, pred[128,128]{1,0:T(8,128)(4,1)S(1)} %copy-done.15), kind=kOutput, calls=%fused_computation.56 | convolution fusion | flops 134283264 | bytes 3293184 | tf_op jit(solution)/shard_map/bij,bjc->bic/dot_general | solution.py:58
  99.6 1.9 %fusion.42 = f32[4,128,1024]{1,2,0:T(8,128)} fusion(bf16[4,128,1024]{2,1,0:T(8,128)(2,1)S(1)} %bitcast.190, bf16[4,128,128]{2,1,0:T(8,128)(2,1)S(1)} %convolution_convert_fusion.1, pred[128,128]{1,0:T(8,128)(4,1)S(1)} %copy-done.14), kind=kOutput, calls=%fused_computation.58 | convolution fusion | flops 134283264 | bytes 3293184 | tf_op jit(solution)/shard_map/bij,bjc->bic/dot_general | solution.py:58
  101.5 1.9 %fusion.44 = f32[4,128,1024]{1,2,0:T(8,128)} fusion(bf16[4,128,1024]{2,1,0:T(8,128)(2,1)S(1)} %bitcast.191, bf16[4,128,128]{2,1,0:T(8,128)(2,1)S(1)} %convolution_convert_fusion.1, pred[128,128]{1,0:T(8,128)(4,1)S(1)} %copy-done.13), kind=kOutput, calls=%fused_computation.60 | convolution fusion | flops 134283264 | bytes 3293184 | tf_op jit(solution)/shard_map/bij,bjc->bic/dot_general | solution.py:58
  103.4 1.8 %fusion.46 = f32[4,128,1024]{1,2,0:T(8,128)} fusion(bf16[4,128,1024]{2,1,0:T(8,128)(2,1)S(1)} %bitcast.192, bf16[4,128,128]{2,1,0:T(8,128)(2,1)S(1)} %convolution_convert_fusion.1, pred[128,128]{1,0:T(8,128)(4,1)S(1)} %copy-done.16), kind=kOutput, calls=%fused_computation.62 | convolution fusion | flops 134283264 | bytes 3293184 | tf_op jit(solution)/shard_map/bij,bjc->bic/dot_general | solution.py:58
  105.3 1.4 fusion.13
  106.7 7.9 %multiply_add_fusion = f32[2,2,128,16,64]{2,4,3,1,0:T(8,128)S(1)} fusion(f32[2,2,128,16,64]{2,4,3,1,0:T(8,128)S(1)} %bitcast.198, f32[2,2,128,16,64]{2,4,3,1,0:T(8,128)} %bitcast.199, f32[2,2,128,16,64]{2,4,3,1,0:T(8,128)} %bitcast.200, f32[2,2,128,16,64]{2,4,3,1,0:T(8,128)} %bitcast.201, f32[2,2,128,16,64]{2,4,3,1,0:T(8,128)} %bitcast.202, ...), kind=kLoop, calls=%fused_computation.7 | loop fusion | flops 7864320 | bytes 19136512 | tf_op jit(solution)/shard_map/add | solution.py:60
  114.9 3.2 %copy.41 = f32[2,2,128,16,64]{2,1,4,3,0:T(2,128)} copy(f32[2,2,128,16,64]{2,4,3,1,0:T(8,128)S(1)} %fusion.14) | data formatting | bytes 4194304 | tf_op jit(solution)/shard_map/scatter-add | solution.py:74
  118.1 2.9 %reshape_reshape.3 = f32[1,2,256,16,64]{2,4,3,1,0:T(8,128)S(1)} reshape(f32[2,2,128,16,64]{2,1,4,3,0:T(2,128)} %copy.41) | data formatting | bytes 4194304 | tf_op jit(solution)/shard_map/reshape;reshape | solution.py:74
  124.2 1.6 copy.44
  126.1 7.8 %collective-permute-done.3 = f32[128,1024]{0,1:T(8,128)} collective-permute-done((f32[128,1024]{0,1:T(8,128)}, f32[128,1024]{0,1:T(8,128)}, u32[]{:S(2)}, u32[]{:S(2)}) %collective-permute-start.3) | collective-permute-done | bytes 524320 | tf_op jit(solution)/shard_map/ppermute | solution.py:14
  136.6 10.0 %collective-permute-done.4 = f32[128,1024]{0,1:T(8,128)S(1)} collective-permute-done((f32[128,1024]{0,1:T(8,128)S(1)}, f32[128,1024]{0,1:T(8,128)S(1)}, u32[]{:S(2)}, u32[]{:S(2)}) %collective-permute-start.4) | collective-permute-done | bytes 524320 | tf_op jit(solution)/shard_map/ppermute | solution.py:14
  146.7 3.0 %collective-permute-start.5 = (f32[128,1024]{0,1:T(8,128)S(1)}, f32[128,1024]{0,1:T(8,128)S(1)}, u32[]{:S(2)}, u32[]{:S(2)}) collective-permute-start(f32[128,1024]{0,1:T(8,128)S(1)} %add.384), channel_id=1, source_target_pairs={{0,16},{16,0},{4,20},{20,4},{8,24},{24,8},{12,28},{28,12},{1,17},{... | collective-permute-start | bytes 1572872 | tf_op jit(solution)/shard_map/ppermute | solution.py:14
  150.6 20.2 %collective-permute-done.5 = f32[128,1024]{0,1:T(8,128)S(1)} collective-permute-done((f32[128,1024]{0,1:T(8,128)S(1)}, f32[128,1024]{0,1:T(8,128)S(1)}, u32[]{:S(2)}, u32[]{:S(2)}) %collective-permute-start.5) | collective-permute-done | bytes 524320 | tf_op jit(solution)/shard_map/ppermute | solution.py:14
  172.0 1.3 copy.45
  (94 shorter events, 29.0 us)
Async XLA Ops:
  6.5 20.4 %copy-start = (bf16[512,128]{1,0:T(8,128)(2,1)S(1)}, bf16[512,128]{1,0:T(8,128)(2,1)}, u32[]{:S(2)}) copy-start(bf16[512,128]{1,0:T(8,128)(2,1)} %param.11) | copy-start | bytes 393220
  6.5 20.4 %copy-start.4 = (bf16[512,128]{1,0:T(8,128)(2,1)S(1)}, bf16[512,128]{1,0:T(8,128)(2,1)}, u32[]{:S(2)}) copy-start(bf16[512,128]{1,0:T(8,128)(2,1)} %param.12) | copy-start | bytes 393220
  6.5 78.5 %all-gather.2.cloned.1.call-start = ((), (), s32[]{:S(2)}) async-start(), calls=%async_computation | async-start | bytes 4718592 | tf_op jit(solution)/shard_map/all_gather | solution.py:34
  7.3 10.2 %collective-permute-start = (bf16[512,512]{1,0:T(8,128)(2,1)}, bf16[512,512]{1,0:T(8,128)(2,1)S(1)}, u32[]{:S(2)}, u32[]{:S(2)}) collective-permute-start(bf16[512,512]{1,0:T(8,128)(2,1)} %param.9), channel_id=1, source_target_pairs={{0,1},{1,2},{2,3},{3,0},{4,5},{5,6},{6,7},{7,4},{8,9},{9,10},{10,1... | collective-permute-start | bytes 1572872 | tf_op jit(solution)/shard_map/ppermute | solution.py:20
  13.3 24.4 %copy-start.3 = (bf16[512,512]{1,0:T(8,128)(2,1)S(1)}, bf16[512,512]{1,0:T(8,128)(2,1)}, u32[]{:S(2)}) copy-start(bf16[512,512]{1,0:T(8,128)(2,1)} %param.9) | copy-start | bytes 1572868
  17.4 8.8 %collective-permute-start.1 = (bf16[512,512]{1,0:T(8,128)(2,1)S(1)}, bf16[512,512]{1,0:T(8,128)(2,1)S(1)}, u32[]{:S(2)}, u32[]{:S(2)}) collective-permute-start(bf16[512,512]{1,0:T(8,128)(2,1)S(1)} %collective-permute-done), channel_id=1, source_target_pairs={{0,1},{1,2},{2,3},{3,0},{4,5},{5,6},{6,7},{7,4},{8,9},{9,10},{10,1... | collective-permute-start | bytes 1572872 | tf_op jit(solution)/shard_map/ppermute | solution.py:20
  26.2 8.6 %collective-permute-start.2 = (bf16[512,512]{1,0:T(8,128)(2,1)S(1)}, bf16[512,512]{1,0:T(8,128)(2,1)S(1)}, u32[]{:S(2)}, u32[]{:S(2)}) collective-permute-start(bf16[512,512]{1,0:T(8,128)(2,1)S(1)} %collective-permute-done.1), channel_id=1, source_target_pairs={{0,1},{1,2},{2,3},{3,0},{4,5},{5,6},{6,7},{7,4},{8,9},{9,10},{10,1... | collective-permute-start | bytes 1572872 | tf_op jit(solution)/shard_map/ppermute | solution.py:20
  85.0 6.5 %copy-start.12 = (pred[128,128]{1,0:T(8,128)(4,1)S(1)}, pred[128,128]{1,0:T(8,128)(4,1)}, u32[]{:S(2)}) copy-start(pred[128,128]{1,0:T(8,128)(4,1)} %fusion.63) | copy-start | bytes 49156
  90.2 1.8 %copy-start.11 = (pred[128,128]{1,0:T(8,128)(4,1)S(1)}, pred[128,128]{1,0:T(8,128)(4,1)}, u32[]{:S(2)}) copy-start(pred[128,128]{1,0:T(8,128)(4,1)} %fusion.64) | copy-start | bytes 49156
  92.0 1.9 %copy-start.10 = (pred[128,128]{1,0:T(8,128)(4,1)S(1)}, pred[128,128]{1,0:T(8,128)(4,1)}, u32[]{:S(2)}) copy-start(pred[128,128]{1,0:T(8,128)(4,1)} %fusion.65) | copy-start | bytes 49156
  93.9 1.8 %copy-start.9 = (pred[128,128]{1,0:T(8,128)(4,1)S(1)}, pred[128,128]{1,0:T(8,128)(4,1)}, u32[]{:S(2)}) copy-start(pred[128,128]{1,0:T(8,128)(4,1)} %fusion.66) | copy-start | bytes 49156
  95.7 1.9 %copy-start.15 = (pred[128,128]{1,0:T(8,128)(4,1)S(1)}, pred[128,128]{1,0:T(8,128)(4,1)}, u32[]{:S(2)}) copy-start(pred[128,128]{1,0:T(8,128)(4,1)} %fusion.67) | copy-start | bytes 49156
  97.6 1.9 %copy-start.14 = (pred[128,128]{1,0:T(8,128)(4,1)S(1)}, pred[128,128]{1,0:T(8,128)(4,1)}, u32[]{:S(2)}) copy-start(pred[128,128]{1,0:T(8,128)(4,1)} %fusion.68) | copy-start | bytes 49156
  99.6 1.9 %copy-start.13 = (pred[128,128]{1,0:T(8,128)(4,1)S(1)}, pred[128,128]{1,0:T(8,128)(4,1)}, u32[]{:S(2)}) copy-start(pred[128,128]{1,0:T(8,128)(4,1)} %fusion.69) | copy-start | bytes 49156
  101.5 1.9 %copy-start.16 = (pred[128,128]{1,0:T(8,128)(4,1)S(1)}, pred[128,128]{1,0:T(8,128)(4,1)}, u32[]{:S(2)}) copy-start(pred[128,128]{1,0:T(8,128)(4,1)} %fusion.70) | copy-start | bytes 49156
  106.7 7.9 %copy-start.1 = (f32[2,128,1024]{1,2,0:T(8,128)S(1)}, f32[2,128,1024]{1,2,0:T(8,128)}, u32[]{:S(2)}) copy-start(f32[2,128,1024]{1,2,0:T(8,128)} %fusion.13) | copy-start | bytes 3145732
  106.7 7.9 %copy-start.8 = (f32[2,128,16]{1,2,0:T(8,128)S(1)}, f32[2,128,16]{1,2,0:T(8,128)}, u32[]{:S(2)}) copy-start(f32[2,128,16]{1,2,0:T(8,128)} %fusion.87) | copy-start | bytes 49156
  121.0 12.8 %collective-permute-start.3 = (f32[128,1024]{0,1:T(8,128)}, f32[128,1024]{0,1:T(8,128)}, u32[]{:S(2)}, u32[]{:S(2)}) collective-permute-start(f32[128,1024]{0,1:T(8,128)} %convolution_bitcast_fusion), channel_id=1, source_target_pairs={{0,4},{4,0},{8,12},{12,8},{16,20},{20,16},{24,28},{28,24},{1,5},{5... | collective-permute-start | bytes 1572872 | tf_op jit(solution)/shard_map/ppermute | solution.py:14
  125.9 8.0 %copy-start.2 = (f32[128,1024]{0,1:T(8,128)S(1)}, f32[128,1024]{0,1:T(8,128)}, u32[]{:S(2)}) copy-start(f32[128,1024]{0,1:T(8,128)} %convolution_bitcast_fusion) | copy-start | bytes 1572868
  135.0 11.6 %collective-permute-start.4 = (f32[128,1024]{0,1:T(8,128)S(1)}, f32[128,1024]{0,1:T(8,128)S(1)}, u32[]{:S(2)}, u32[]{:S(2)}) collective-permute-start(f32[128,1024]{0,1:T(8,128)S(1)} %add.379), channel_id=1, source_target_pairs={{0,8},{8,0},{4,12},{12,4},{16,24},{24,16},{20,28},{28,20},{1,9},{9... | collective-permute-start | bytes 1572872 | tf_op jit(solution)/shard_map/ppermute | solution.py:14
  146.7 24.1 %collective-permute-start.5 = (f32[128,1024]{0,1:T(8,128)S(1)}, f32[128,1024]{0,1:T(8,128)S(1)}, u32[]{:S(2)}, u32[]{:S(2)}) collective-permute-start(f32[128,1024]{0,1:T(8,128)S(1)} %add.384), channel_id=1, source_target_pairs={{0,16},{16,0},{4,20},{20,4},{8,24},{24,8},{12,28},{28,12},{1,17},{... | collective-permute-start | bytes 1572872 | tf_op jit(solution)/shard_map/ppermute | solution.py:14
  150.1 21.1 %copy-start.5 = (f32[512,16]{0,1:T(8,128)S(1)}, f32[512,16]{0,1:T(8,128)}, u32[]{:S(2)}) copy-start(f32[512,16]{0,1:T(8,128)} %get-tuple-element.29) | copy-start | bytes 98308
  150.1 21.1 %copy-start.6 = (f32[512,16]{0,1:T(8,128)S(1)}, f32[512,16]{0,1:T(8,128)}, u32[]{:S(2)}) copy-start(f32[512,16]{0,1:T(8,128)} %get-tuple-element.40) | copy-start | bytes 98308
  150.1 21.1 %copy-start.7 = (f32[512,16]{0,1:T(8,128)S(1)}, f32[512,16]{0,1:T(8,128)}, u32[]{:S(2)}) copy-start(f32[512,16]{0,1:T(8,128)} %get-tuple-element.41) | copy-start | bytes 98308
Sparse Core Ops, SparseCore 0:
  9.5 75.5 all-gather.1
